TPU v7x, 256 devices: a whole 4x4x8 slice. The times are simulated.
256 devices in a mesh: req: 32 (over y, x, z_hi), tp: 8 (over z_lo, core).
Axes of the slice: x: 4, y: 4, z: 8 (z_hi: 2, z_lo: 4; z = z_hi * 4 + z_lo), core: 2. Of those that a mesh axis runs over, the one named last changes fastest.
Arguments:
- residual: bfloat16 [8192, 2304], P('req'), may hold values from -58 to 58
- context: bfloat16 [8192, 2304], P('req', 'tp'), may hold values from -6 to 6
- attention_output_weight: bfloat16 [2304, 2304], P('tp'), may hold values from -0.1875 to 0.1875
- adapter_down_maps: bfloat16 [64, 2304, 16], P('req', 'tp'), may hold values from -0.125 to 0.125
- adapter_up_maps: bfloat16 [64, 16, 2304], P('req'), may hold values from -1.5 to 1.5
- adapter_storage_row: int32 [64], replicated, may hold values from 0 to 63, each once
- active_adapters: int32 [16], replicated, may hold values from 0 to 63, as said below
- request_token_length: int32 [32, 4], P('req'), may hold values from 1 to 128, 256 in all within a row
- request_adapter_entry: int32 [32, 4], P('req'), may hold values from 0 to 15
- expert_norm_gain: bfloat16 [2304], replicated, may hold values from 0.099609375 to 1.8984375
- router_projection: bfloat16 [2304, 8], replicated, may hold values from -0.125 to 0.125
- expert_choice_pairs: int32 [8192, 2], P('req'), may hold values from 0 to 7, all different within a row; in each aligned block of 256 rows (0 to 255, 256 to 511, ...) at most 80 rows name the same one
- expert_gate_weight: bfloat16 [32, 2304, 5760], P('req', None, 'tp'), as said below
- expert_up_weight: bfloat16 [32, 2304, 5760], P('req', None, 'tp'), as said below
- expert_down_weight: bfloat16 [32, 5760, 2304], P('req', 'tp'), as said below
Outputs:
- layer_out: bfloat16 [8192, 2304], P('req', 'tp')
Inputs may be any that keep to these rules, and one draw needn't show every extreme that they name: `active_adapters`: 16 different adapter numbers, 0 and 63 among them. `adapter_storage_row`: every stored row appears once. `request_token_length`: each group's lengths sum to 256; the longest request of a group has exactly half of 256 tokens. `expert_choice_pairs`: each row names two different experts; within the 256 rows of one group no expert is named by more than 80 rows, a bound that some block reaches. `expert_gate_weight`: the 4 holders c * 8 + e of expert e hold the same weights. `expert_up_weight`: the 4 holders c * 8 + e of expert e hold the same weights. `expert_down_weight`: the 4 holders c * 8 + e of expert e hold the same weights.
All inputs are finite; a program needn't handle non-finite values.
Results may differ from a plain program's by a relative error of at most 0.0095.
Values may be sent and summed in bfloat16 or wider, within the bound.
A program may use at most 128 MiB of HBM per device.

v0:
```python
import jax
import jax.numpy as jnp
from jax import lax
from jax.sharding import Mesh
from jax.sharding import PartitionSpec as P

CAP = 80
NORM_EPS = 1e-05
REQ = ("ry", "rxz")


def segment_onehot(request_token_length, token_count):
    bounds = jnp.cumsum(request_token_length[0])
    position = jnp.arange(token_count, dtype=jnp.int32)
    segment = jnp.sum((position[:, None] >= bounds[None, :]).astype(jnp.int32), axis=1)
    slot_range = jnp.arange(request_token_length.shape[1], dtype=jnp.int32)
    return segment[:, None] == slot_range[None, :]


def route_tables(expert_choice_pairs, expert_count, capacity):
    expert_ids = jnp.arange(expert_count, dtype=jnp.int32)
    first_hit = expert_choice_pairs[None, :, 0] == expert_ids[:, None]
    second_hit = expert_choice_pairs[None, :, 1] == expert_ids[:, None]
    chosen = first_hit | second_hit
    slot_of = jnp.cumsum(chosen.astype(jnp.int32), axis=1) - 1
    slot_range = jnp.arange(capacity, dtype=jnp.int32)
    placement = chosen[:, None, :] & (slot_of[:, None, :] == slot_range[None, :, None])
    return (placement, first_hit, second_hit)


def on_device(
    residual,
    context,
    attention_output_weight,
    adapter_down_maps,
    adapter_up_maps,
    adapter_storage_row,
    active_adapters,
    request_token_length,
    request_adapter_entry,
    expert_norm_gain,
    router_projection,
    expert_choice_pairs,
    expert_gate_weight,
    expert_up_weight,
    expert_down_weight,
):
    token_count = residual.shape[0]
    hidden_width = residual.shape[1]
    feature_share = context.shape[1]
    local_rows = adapter_down_maps.shape[0]
    adapter_rank_size = adapter_down_maps.shape[2]
    request_count = request_token_length.shape[1]
    share_width = hidden_width // lax.axis_size("tp")
    share_start = lax.axis_index("tp") * share_width
    up_slice = lax.dynamic_slice_in_dim(adapter_up_maps, share_start, share_width, 2)
    packed = jnp.concatenate(
        [
            adapter_down_maps.reshape(local_rows, feature_share * adapter_rank_size),
            up_slice.reshape(local_rows, adapter_rank_size * share_width),
        ],
        axis=1,
    )
    all_packed = lax.all_gather(packed, REQ, axis=0, tiled=True)
    request_rows = adapter_storage_row[active_adapters[request_adapter_entry[0]]]
    picked = all_packed[request_rows]
    down_req = picked[:, : feature_share * adapter_rank_size].reshape(
        request_count, feature_share, adapter_rank_size
    )
    up_req = picked[:, feature_share * adapter_rank_size :].reshape(
        request_count * adapter_rank_size, share_width
    )
    down_joined = jnp.transpose(down_req, (1, 0, 2)).reshape(
        feature_share, request_count * adapter_rank_size
    )
    segment_hot = segment_onehot(request_token_length, token_count)
    low_all = jnp.dot(context, down_joined, preferred_element_type=jnp.float32)
    reduced_mask = jnp.repeat(segment_hot, adapter_rank_size, axis=1)
    low_part = jnp.where(reduced_mask, low_all, 0.0)
    low_total = lax.psum(low_part, "tp").astype(jnp.bfloat16)
    lora_share = jnp.dot(low_total, up_req, preferred_element_type=jnp.float32)
    base = jnp.dot(context, attention_output_weight, preferred_element_type=jnp.float32)
    base_share = lax.dynamic_slice_in_dim(base, share_start, share_width, 1)
    head_part = lax.dynamic_update_slice_in_dim(base, base_share + lora_share, share_start, 1)
    gain_all = expert_norm_gain.astype(jnp.float32)
    head_sum = lax.psum(head_part.astype(jnp.bfloat16), "tp").astype(jnp.float32)
    blended_rows = residual.astype(jnp.float32) + head_sum
    mean_square = jnp.mean(blended_rows * blended_rows, axis=1, keepdims=True)
    normed = (blended_rows * lax.rsqrt(mean_square + NORM_EPS) * gain_all).astype(jnp.bfloat16)
    mixed_share = lax.dynamic_slice_in_dim(blended_rows, share_start, share_width, 1)
    logits = jnp.dot(normed, router_projection, preferred_element_type=jnp.float32)
    expert_count = router_projection.shape[1]
    expert_range = jnp.arange(expert_count, dtype=jnp.int32)
    logit_first = jnp.sum(
        jnp.where(expert_choice_pairs[:, 0:1] == expert_range[None, :], logits, 0.0), axis=1
    )
    logit_second = jnp.sum(
        jnp.where(expert_choice_pairs[:, 1:2] == expert_range[None, :], logits, 0.0), axis=1
    )
    weight_first = 1.0 / (1.0 + jnp.exp(logit_second - logit_first))
    weight_second = 1.0 / (1.0 + jnp.exp(logit_first - logit_second))
    placement, first_hit, second_hit = route_tables(expert_choice_pairs, expert_count, CAP)
    send_rows = jnp.einsum(
        "est,td->esd", placement.astype(jnp.bfloat16), normed, preferred_element_type=jnp.float32
    ).astype(jnp.bfloat16)
    rows_in = lax.all_to_all(send_rows, "rxz", split_axis=0, concat_axis=0, tiled=True)
    rows_flat = rows_in.reshape(expert_count * CAP, hidden_width)
    gate_value = jnp.dot(rows_flat, expert_gate_weight[0], preferred_element_type=jnp.float32)
    up_value = jnp.dot(rows_flat, expert_up_weight[0], preferred_element_type=jnp.float32)
    hidden = (jax.nn.silu(gate_value) * up_value).astype(jnp.bfloat16)
    partial_value = jnp.dot(hidden, expert_down_weight[0], preferred_element_type=jnp.float32)
    returned = lax.all_to_all(
        partial_value.astype(jnp.bfloat16).reshape(expert_count, CAP, hidden_width),
        "rxz",
        split_axis=0,
        concat_axis=0,
        tiled=True,
    )
    token_weight = jnp.where(first_hit, weight_first[None, :], 0.0) + jnp.where(
        second_hit, weight_second[None, :], 0.0
    )
    scaled_place = placement.astype(jnp.float32) * token_weight[:, None, :]
    contribution = jnp.einsum(
        "est,esd->td",
        scaled_place,
        returned.astype(jnp.float32),
        precision=lax.Precision.HIGHEST,
        preferred_element_type=jnp.float32,
    )
    moe_share = lax.psum_scatter(
        contribution.astype(jnp.bfloat16), "tp", scatter_dimension=1, tiled=True
    ).astype(jnp.float32)
    return (mixed_share + moe_share).astype(jnp.bfloat16)


def solution(mesh):
    req_size = mesh.shape["req"]
    plane = 8
    split_mesh = Mesh(
        mesh.devices.reshape(req_size // plane, plane, mesh.shape["tp"]), ("ry", "rxz", "tp")
    )
    return jax.shard_map(
        on_device,
        mesh=split_mesh,
        in_specs=(
            P(REQ, None),
            P(REQ, "tp"),
            P("tp", None),
            P(REQ, "tp", None),
            P(REQ, None, None),
            P(),
            P(),
            P(REQ, None),
            P(REQ, None),
            P(),
            P(),
            P(REQ, None),
            P(REQ, None, "tp"),
            P(REQ, None, "tp"),
            P(REQ, "tp", None),
        ),
        out_specs=P(REQ, "tp"),
        check_vma=False,
    )
```

profile of v0, /device:TPU:4, one launch (start us, length us, event | category | flops | bytes accessed | tf_op | source)
XLA Modules:
  0.0 434.4 jit_solution(16234100951384589022)
XLA Ops:
  6.5 0.0 copy-start
  6.5 0.0 all-gather.3.cloned.1.call-start
  6.5 1.0 constant_dynamic-slice_fusion
  7.5 0.1 reshape.268
  7.6 0.9 copy.29
  8.5 0.2 reshape.267
  8.7 0.7 maximum_bitcast_fusion
  9.3 0.0 all-gather.3.cloned.1.call-update
  9.4 0.0 all-reduce.2.cloned.1.call-start
  9.4 0.8 reduce-window.18
  10.2 0.7 fusion.27
  10.9 1.3 gather_fusion
  12.2 1.3 gather_fusion.1
  13.5 0.1 convert_reduce_fusion
  13.6 3.6 fusion.35
  17.2 0.0 copy-start.4
  17.2 77.7 %all-gather.3.cloned.1.call-done = bf16[32,2,9216]{2,1,0:T(2,128)(2,1)} async-done(((bf16[1,2,9216]{2,1,0:T(2,128)(2,1)}), bf16[32,2,9216]{2,1,0:T(2,128)(2,1)}) %all-gather.3.cloned.1.call-update) | async-done | bytes 1179664 | tf_op jit(solution)/shard_map/all_gather | solution.py:64
  94.9 2.3 reshape.300
  97.3 2.1 gather_fusion.2
  99.4 0.6 fusion.33
  100.0 1.5 reshape.271
  101.5 1.7 reshape.269
  103.3 1.7 copy.30
  105.0 0.0 copy-done.4
  105.0 1.0 fusion.10
  106.0 26.3 %psum.14 = bf16[256,64]{0,1:T(8,128)(2,1)S(1)} all-reduce(f32[256,64]{0,1:T(8,128)S(1)} %fusion.10), channel_id=1, replica_groups=mesh['ry'=4,'rxz'=8,'tp'=8] {'tp'}, use_global_device_ids=true, to_apply=%region_2.3 | all-reduce | flops 16384 | bytes 98304 | tf_op jit(solution)/shard_map/psum | solution.py:80
  132.3 2.1 convolution_add_fusion
  134.4 3.5 dynamic_update_slice.3
  137.9 0.0 copy-start.6
  137.9 0.0 copy-start.5
  137.9 2.8 convert_element_type.49
  140.7 0.0 all-reduce.2.cloned.1.call-update
  140.7 0.0 copy-done.6
  140.8 0.6 reduce-window.19
  141.3 0.2 slice_reduce_fusion
  141.6 0.0 copy-done.5
  141.6 0.1 add_bitcast_fusion
  141.7 69.1 %all-reduce.2.cloned.1.call-done = bf16[256,2304]{1,0:T(8,128)(2,1)} async-done(((bf16[256,2304]{1,0:T(8,128)(2,1)}), bf16[256,2304]{1,0:T(8,128)(2,1)}) %all-reduce.2.cloned.1.call-update) | async-done | bytes 1179664 | tf_op jit(solution)/shard_map/psum | solution.py:86
  210.8 0.0 copy-start.1
  210.8 0.0 copy-start.2
  210.8 3.6 convert_add_fusion
  214.4 0.0 copy-done.1
  214.4 0.0 copy-done.2
  214.4 1.2 convolution_convert_fusion.1
  215.6 0.0 copy-start.7
  215.6 74.4 %all_to_all.10 = bf16[8,80,2304]{2,1,0:T(8,128)(2,1)S(1)} all-to-all(bf16[8,80,2304]{2,1,0:T(8,128)(2,1)S(1)} %convolution_convert_fusion.1), channel_id=1, replica_groups=mesh['ry'=4,'rxz'=8,'tp'=8] {'rxz'}, dimensions={0} | all-to-all | bytes 5898240 | tf_op jit(solution)/shard_map/all_to_all | solution.py:106
  290.0 0.0 copy-start.3
  290.0 1.6 copy-done.3
  291.7 0.0 copy-done.7
  291.7 4.0 fusion.5
  295.6 0.0 copy-done
  295.6 14.5 %convolution_convert_fusion = bf16[640,2304]{1,0:T(8,128)(2,1)} fusion(bf16[1,720,2304]{2,1,0:T(8,128)(2,1)S(1)} %copy-done, f32[640,720]{0,1:T(8,128)} %fusion.5, bf16[640,2304]{1,0:T(8,128)(2,1)} %bitcast.68, bf16[1,2304,720]{1,2,0:T(8,128)(2,1)} %param.28), kind=kOutput, calls=%fused_computation.3 | convolution fusion | flops 4250972160 | bytes 14376960 | tf_op jit(solution)/shard_map/dot_general | solution.py:111
  310.1 0.0 copy-start.8
  310.2 7.4 %all-to-all-start.1 = ((bf16[8,80,2304]{2,1,0:T(8,128)(2,1)}), bf16[8,80,2304]{2,1,0:T(8,128)(2,1)}, u32[]{:S(2)}, u32[]{:S(2)}) async-start(bf16[8,80,2304]{2,1,0:T(8,128)(2,1)} %bitcast.66), calls=%async_computation.1 | async-start | bytes 5898240 | tf_op jit(solution)/shard_map/all_to_all | solution.py:112
  317.5 0.0 reduce-scatter.4.cloned.1.call-start
  317.5 0.0 copy-done.8
  317.5 2.2 select_reduce_fusion.1
  319.8 57.1 %all-to-all-done.1 = bf16[8,80,2304]{2,1,0:T(8,128)(2,1)} async-done(((bf16[8,80,2304]{2,1,0:T(8,128)(2,1)}), bf16[8,80,2304]{2,1,0:T(8,128)(2,1)}, u32[]{:S(2)}, u32[]{:S(2)}) %all-to-all-start.1) | async-done | bytes 2949152 | tf_op jit(solution)/shard_map/all_to_all | solution.py:112
  376.9 6.4 %fusion.1 = bf16[2304,256]{1,0:T(8,128)(2,1)} fusion(bf16[8,80,2304]{2,1,0:T(8,128)(2,1)} %all-to-all-done.1, f32[8,256]{1,0:T(8,128)S(1)} %select_add_fusion, s32[8,256]{1,0:T(8,128)S(1)} %add_bitcast_fusion, pred[8,256]{1,0:T(8,128)(4,1)S(1)} %fusion.24), kind=kOutput, calls=%fused_computation.7 | convolution fusion | flops 4530929664 | bytes 4147200 | tf_op jit(solution)/shard_map/est,esd->td/dot_general | solution.py:123
  383.3 0.0 reduce-scatter.4.cloned.1.call-update
  383.3 39.9 %reduce-scatter.4.cloned.1.call-done = bf16[288,256]{1,0:T(8,128)(2,1)} async-done(((bf16[2304,256]{1,0:T(8,128)(2,1)}), bf16[288,256]{1,0:T(8,128)(2,1)}) %reduce-scatter.4.cloned.1.call-update) | async-done | bytes 147472
  423.2 1.1 copy.36
  424.3 1.9 add_convert_fusion
  426.2 1.7 copy.33
  (16 shorter events, 0.1 us)
Async XLA Ops:
  6.5 289.1 %copy-start = (bf16[1,720,2304]{2,1,0:T(8,128)(2,1)S(1)}, bf16[1,720,2304]{2,1,0:T(8,128)(2,1)}, u32[]{:S(2)}) copy-start(bf16[1,720,2304]{2,1,0:T(8,128)(2,1)} %param.29) | copy-start | bytes 9953284
  6.5 88.4 %all-gather.3.cloned.1.call-start = ((), (), s32[]{:S(2)}) async-start(), calls=%async_computation.4 | async-start | bytes 1216512 | tf_op jit(solution)/shard_map/all_gather | solution.py:64
  9.4 201.5 %all-reduce.2.cloned.1.call-start = ((), (), s32[]{:S(2)}) async-start(), calls=%async_computation.3 | async-start | bytes 2359296 | tf_op jit(solution)/shard_map/psum | solution.py:86
  17.2 87.8 %copy-start.4 = (bf16[256,288]{0,1:T(8,128)(2,1)S(1)}, bf16[256,288]{0,1:T(8,128)(2,1)}, u32[]{:S(2)}) copy-start(bf16[256,288]{0,1:T(8,128)(2,1)} %param.16) | copy-start | bytes 442372
  137.9 2.8 copy-start.6
  137.9 3.7 copy-start.5
  210.8 3.6 copy-start.1
  210.8 3.6 copy-start.2
  215.6 76.1 %copy-start.7 = (bf16[1,2304,720]{1,2,0:T(8,128)(2,1)S(1)}, bf16[1,2304,720]{1,2,0:T(8,128)(2,1)}, u32[]{:S(2)}) copy-start(bf16[1,2304,720]{1,2,0:T(8,128)(2,1)} %param.27) | copy-start | bytes 9953284
  290.0 1.6 copy-start.3
  310.1 7.4 %copy-start.8 = (bf16[2304,8]{0,1:T(8,128)(2,1)S(1)}, bf16[2304,8]{0,1:T(8,128)(2,1)}, u32[]{:S(2)}) copy-start(bf16[2304,8]{0,1:T(8,128)(2,1)} %param.25) | copy-start | bytes 110596
  310.2 66.7 %all-to-all-start.1 = ((bf16[8,80,2304]{2,1,0:T(8,128)(2,1)}), bf16[8,80,2304]{2,1,0:T(8,128)(2,1)}, u32[]{:S(2)}, u32[]{:S(2)}) async-start(bf16[8,80,2304]{2,1,0:T(8,128)(2,1)} %bitcast.66), calls=%async_computation.1 | async-start | bytes 5898240 | tf_op jit(solution)/shard_map/all_to_all | solution.py:112
  317.5 105.7 %reduce-scatter.4.cloned.1.call-start = ((), (), s32[]{:S(2)}) async-start(), calls=%async_computation.5 | async-start | bytes 1327104
Sparse Core Ops, SparseCore 0:
  10.8 84.0 all-gather.2
  140.8 69.9 all-reduce.1
  383.4 39.7 reduce-scatter.3
where the time goes:
time: 435 us; the launch traced here: 434 us
  waiting for transfers between devices  244 us (56%)
  blocking collectives  101 us (23%)
  matrix products  34.9 us (8%)
  local copies, waits for them, and re-layouts  22.9 us (5%)
  between operations  13.2 us (3%)
  other arithmetic  11.3 us (3%)
  starting transfers between devices  7.41 us (2%)
    all_gather x1, waiting for transfers between devices, on_device(): all_packed = lax.all_gather(packed, REQ, axis=0, tiled=True)  77.7 us
    all_to_all x1, blocking collectives, on_device(): lax.all_to_all(send_rows, 'rxz', split_axis=0, concat_axis=0, tiled=True)  74.4 us
    psum x1, waiting for transfers between devices, on_device(): lax.psum(head_part.astype(jnp.bfloat16), 'tp').astype(jnp.float32)  69.1 us
    all_to_all x1, waiting for transfers between devices, on_device(): lax.all_to_all(partial_value.astype(jnp.bfloat16).reshape(expert_count, C...  57.1 us
    unnamed x4, waiting for transfers between devices  40 us
    psum x1, blocking collectives, on_device(): low_total = lax.psum(low_part, 'tp').astype(jnp.bfloat16)  26.3 us
    dot_general x1, matrix products, on_device(): jnp.dot(hidden, expert_down_weight[0], preferred_element_type=jnp.float32)  14.5 us
  transfers between devices with their start and end apart: 4, of which 4 were waited for; matrix products, arithmetic and copies ran while one was open for 3% of the time, Pallas kernels for 0%

commit v1 on v0

--- a/solution.py
+++ b/solution.py
@@ -7,6 +7,11 @@
 CAP = 80
 NORM_EPS = 1e-05
 REQ = ("ry", "rxz")
+
+
+def summed_here(x, axis):
+    parts = lax.all_gather(x, axis)
+    return jnp.sum(parts, axis=0)
 
 
 def segment_onehot(request_token_length, token_count):
@@ -83,7 +88,7 @@
     base_share = lax.dynamic_slice_in_dim(base, share_start, share_width, 1)
     head_part = lax.dynamic_update_slice_in_dim(base, base_share + lora_share, share_start, 1)
     gain_all = expert_norm_gain.astype(jnp.float32)
-    head_sum = lax.psum(head_part.astype(jnp.bfloat16), "tp").astype(jnp.float32)
+    head_sum = summed_here(head_part.astype(jnp.bfloat16), "tp").astype(jnp.float32)
     blended_rows = residual.astype(jnp.float32) + head_sum
     mean_square = jnp.mean(blended_rows * blended_rows, axis=1, keepdims=True)
     normed = (blended_rows * lax.rsqrt(mean_square + NORM_EPS) * gain_all).astype(jnp.bfloat16)

time: 435 us -> 469 us (1.078)
  waiting for transfers between devices: 244 us -> 272 us
  other arithmetic: 11.3 us -> 17.5 us
    all_gather x0 -> x1, waiting for transfers between devices: none -> 95.7 us  [summed_here(): parts = lax.all_gather(x, axis)]
    psum x1 -> x0, waiting for transfers between devices: 69.1 us -> none  [on_device(): lax.psum(head_part.astype(jnp.bfloat16), 'tp').astype(jnp.float32)]
    reduce_scatter x0 -> x1, waiting for transfers between devices: none -> 68.3 us  [on_device(): lax.psum_scatter(contribution.astype(jnp.bfloat16), 'tp', scatter_dimensi...]
    unnamed x4 -> x3, waiting for transfers between devices: 40 us -> 0.05 us
    all_to_all x1, waiting for transfers between devices: 57.1 us -> 30.2 us  [on_device(): lax.all_to_all(partial_value.astype(jnp.bfloat16).reshape(expert_count, C...]
    reduce_sum x0 -> x1, other arithmetic: none -> 6.39 us  [summed_here(): return jnp.sum(parts, axis=0)]
where the time goes in v1:
time: 469 us; the launch traced here: 468 us
  waiting for transfers between devices  272 us (58%)
  blocking collectives  101 us (22%)
  matrix products  35 us (7%)
  local copies, waits for them, and re-layouts  24.3 us (5%)
  other arithmetic  17.5 us (4%)
  between operations  13.2 us (3%)
  starting transfers between devices  5.79 us (1%)
    all_gather x1, waiting for transfers between devices, summed_here(): parts = lax.all_gather(x, axis)  95.7 us
    all_gather x1, waiting for transfers between devices, on_device(): all_packed = lax.all_gather(packed, REQ, axis=0, tiled=True)  77.7 us
    all_to_all x1, blocking collectives, on_device(): lax.all_to_all(send_rows, 'rxz', split_axis=0, concat_axis=0, tiled=True)  74.2 us
    reduce_scatter x1, waiting for transfers between devices, on_device(): lax.psum_scatter(contribution.astype(jnp.bfloat16), 'tp', scatter_dimensi...  68.3 us
    all_to_all x1, waiting for transfers between devices, on_device(): lax.all_to_all(partial_value.astype(jnp.bfloat16).reshape(expert_count, C...  30.2 us
    psum x1, blocking collectives, on_device(): low_total = lax.psum(low_part, 'tp').astype(jnp.bfloat16)  26.3 us
    dot_general x1, matrix products, on_device(): jnp.dot(hidden, expert_down_weight[0], preferred_element_type=jnp.float32)  14.5 us
  transfers between devices with their start and end apart: 4, of which 4 were waited for; matrix products, arithmetic and copies ran while one was open for 3% of the time, Pallas kernels for 0%

profile of v1, /device:TPU:4, one launch (start us, length us, event | category | flops | bytes accessed | tf_op | source)
XLA Modules:
  0.0 468.2 jit_solution(10297106777084233211)
XLA Ops:
  6.5 0.0 copy-start
  6.5 0.0 all-gather.7.cloned.1.call-start
  6.5 1.0 constant_dynamic-slice_fusion
  7.5 0.1 reshape.268
  7.6 0.9 copy.31
  8.5 0.2 reshape.267
  8.7 0.7 maximum_bitcast_fusion
  9.3 0.0 all-gather.7.cloned.1.call-update
  9.4 0.0 all-gather.5.cloned.1.call-start
  9.4 0.8 reduce-window.18
  10.2 0.7 fusion.26
  10.9 1.3 gather_fusion
  12.2 1.3 gather_fusion.1
  13.5 0.1 convert_reduce_fusion
  13.6 3.6 fusion.34
  17.2 77.7 %all-gather.7.cloned.1.call-done = bf16[32,2,9216]{2,1,0:T(2,128)(2,1)} async-done(((bf16[1,2,9216]{2,1,0:T(2,128)(2,1)}), bf16[32,2,9216]{2,1,0:T(2,128)(2,1)}) %all-gather.7.cloned.1.call-update) | async-done | bytes 1179664 | tf_op jit(solution)/shard_map/all_gather | solution.py:69
  94.9 2.3 reshape.301
  97.3 2.1 gather_fusion.2
  99.4 0.6 fusion.32
  100.0 1.7 reshape.269
  101.8 1.7 copy.32
  103.5 0.0 copy-done.4
  103.5 1.0 fusion.9
  104.5 26.3 %psum.7 = bf16[256,64]{0,1:T(8,128)(2,1)S(1)} all-reduce(f32[256,64]{0,1:T(8,128)S(1)} %fusion.9), channel_id=1, replica_groups=mesh['ry'=4,'rxz'=8,'tp'=8] {'tp'}, use_global_device_ids=true, to_apply=%region_2.3 | all-reduce | flops 16384 | bytes 98304 | tf_op jit(solution)/shard_map/psum | solution.py:85
  130.8 0.9 reshape.271
  131.7 2.0 convolution_add_fusion
  133.7 3.5 dynamic_update_slice.3
  137.3 2.8 convert_element_type.51
  140.1 0.0 copy-start.5
  140.1 0.0 copy-start.6
  140.1 0.0 all-gather.5.cloned.1.call-update
  140.1 2.4 copy.30
  142.5 0.0 copy-done.5
  142.5 0.0 copy-done.6
  142.5 0.6 reduce-window.19
  143.1 0.2 slice_reduce_fusion
  143.4 0.1 add_bitcast_fusion
  143.4 95.7 %all-gather.5.cloned.1.call-done = bf16[2048,2304]{1,0:T(8,128)(2,1)} async-done(((bf16[256,2304]{1,0:T(8,128)(2,1)}), bf16[2048,2304]{1,0:T(8,128)(2,1)}) %all-gather.5.cloned.1.call-update) | async-done | bytes 9437200 | tf_op jit(solution)/shard_map/all_gather | solution.py:13
  239.1 6.4 %reduce_sum.49 = bf16[256,2304]{1,0:T(8,128)(2,1)} reduce(bf16[8,256,2304]{2,1,0:T(8,128)(2,1)} %bitcast.62, bf16[]{:T(256)} %constant.33.clone.1), dimensions={0}, to_apply=%region_3.4 | reduce | flops 4128768 | bytes 10616834 | tf_op jit(solution)/shard_map/reduce_sum | solution.py:14
  245.5 2.4 copy.34
  247.9 0.0 copy-start.1
  247.9 0.0 copy-start.2
  247.9 3.6 convert_add_fusion
  251.5 0.0 copy-done.1
  251.5 0.0 copy-done.2
  251.5 1.2 convolution_convert_fusion.1
  252.6 0.0 copy-start.7
  252.7 74.2 %all_to_all.10 = bf16[8,80,2304]{2,1,0:T(8,128)(2,1)S(1)} all-to-all(bf16[8,80,2304]{2,1,0:T(8,128)(2,1)S(1)} %convolution_convert_fusion.1), channel_id=1, replica_groups=mesh['ry'=4,'rxz'=8,'tp'=8] {'rxz'}, dimensions={0} | all-to-all | bytes 5898240 | tf_op jit(solution)/shard_map/all_to_all | solution.py:111
  326.9 0.0 copy-start.3
  326.9 1.6 copy-done.3
  328.5 0.0 copy-done.7
  328.5 4.1 fusion.4
  332.6 0.0 copy-done
  332.6 14.5 %convolution_convert_fusion = bf16[640,2304]{1,0:T(8,128)(2,1)} fusion(bf16[1,720,2304]{2,1,0:T(8,128)(2,1)S(1)} %copy-done, f32[640,720]{0,1:T(8,128)} %fusion.4, bf16[640,2304]{1,0:T(8,128)(2,1)} %bitcast.65, bf16[1,2304,720]{1,2,0:T(8,128)(2,1)} %param.28), kind=kOutput, calls=%fused_computation.3 | convolution fusion | flops 4250972160 | bytes 14376960 | tf_op jit(solution)/shard_map/dot_general | solution.py:116
  347.1 0.0 copy-start.8
  347.1 5.7 %all-to-all-start.1 = ((bf16[8,80,2304]{2,1,0:T(8,128)(2,1)}), bf16[8,80,2304]{2,1,0:T(8,128)(2,1)}, u32[]{:S(2)}, u32[]{:S(2)}) async-start(bf16[8,80,2304]{2,1,0:T(8,128)(2,1)} %bitcast.63), calls=%async_computation.1 | async-start | bytes 5898240 | tf_op jit(solution)/shard_map/all_to_all | solution.py:117
  352.8 0.0 reduce-scatter.2.cloned.1.call-start
  352.8 0.0 copy-done.8
  352.8 2.2 select_reduce_fusion.1
  355.1 30.2 %all-to-all-done.1 = bf16[8,80,2304]{2,1,0:T(8,128)(2,1)} async-done(((bf16[8,80,2304]{2,1,0:T(8,128)(2,1)}), bf16[8,80,2304]{2,1,0:T(8,128)(2,1)}, u32[]{:S(2)}, u32[]{:S(2)}) %all-to-all-start.1) | async-done | bytes 2949152 | tf_op jit(solution)/shard_map/all_to_all | solution.py:117
  385.2 6.4 %fusion = bf16[256,2304]{0,1:T(8,128)(2,1)} fusion(bf16[8,80,2304]{2,1,0:T(8,128)(2,1)} %all-to-all-done.1, f32[8,256]{1,0:T(8,128)S(1)} %select_add_fusion, s32[8,256]{1,0:T(8,128)S(1)} %add_bitcast_fusion, pred[8,256]{1,0:T(8,128)(4,1)S(1)} %fusion.23), kind=kOutput, calls=%fused_computation.6 | convolution fusion | flops 4530929664 | bytes 4147200 | tf_op jit(solution)/shard_map/est,esd->td/dot_general | solution.py:128
  391.6 0.0 reduce-scatter.2.cloned.1.call-update
  391.7 68.3 %reduce-scatter.2.cloned.1.call-done = bf16[256,288]{0,1:T(8,128)(2,1)} async-done(((bf16[256,2304]{0,1:T(8,128)(2,1)}), bf16[256,288]{0,1:T(8,128)(2,1)}) %reduce-scatter.2.cloned.1.call-update) | async-done | bytes 147472 | tf_op jit(solution)/shard_map/reduce_scatter | solution.py:135
  459.9 1.7 add_convert_fusion
  (17 shorter events, 0.1 us)
Async XLA Ops:
  6.5 326.1 %copy-start = (bf16[1,720,2304]{2,1,0:T(8,128)(2,1)S(1)}, bf16[1,720,2304]{2,1,0:T(8,128)(2,1)}, u32[]{:S(2)}) copy-start(bf16[1,720,2304]{2,1,0:T(8,128)(2,1)} %param.29) | copy-start | bytes 9953284
  6.5 88.4 %all-gather.7.cloned.1.call-start = ((), (), s32[]{:S(2)}) async-start(), calls=%async_computation.5 | async-start | bytes 1216512 | tf_op jit(solution)/shard_map/all_gather | solution.py:69
  9.4 229.8 %all-gather.5.cloned.1.call-start = ((), (), s32[]{:S(2)}) async-start(), calls=%async_computation.4 | async-start | bytes 10616832 | tf_op jit(solution)/shard_map/all_gather | solution.py:13
  17.2 86.2 %copy-start.4 = (bf16[256,288]{0,1:T(8,128)(2,1)S(1)}, bf16[256,288]{0,1:T(8,128)(2,1)}, u32[]{:S(2)}) copy-start(bf16[256,288]{0,1:T(8,128)(2,1)} %param.16) | copy-start | bytes 442372
  140.1 2.4 copy-start.5
  140.1 2.4 copy-start.6
  247.9 3.6 copy-start.1
  247.9 3.6 copy-start.2
  252.6 75.9 %copy-start.7 = (bf16[1,2304,720]{1,2,0:T(8,128)(2,1)S(1)}, bf16[1,2304,720]{1,2,0:T(8,128)(2,1)}, u32[]{:S(2)}) copy-start(bf16[1,2304,720]{1,2,0:T(8,128)(2,1)} %param.27) | copy-start | bytes 9953284
  326.9 1.6 copy-start.3
  347.1 5.8 %copy-start.8 = (bf16[2304,8]{0,1:T(8,128)(2,1)S(1)}, bf16[2304,8]{0,1:T(8,128)(2,1)}, u32[]{:S(2)}) copy-start(bf16[2304,8]{0,1:T(8,128)(2,1)} %param.25) | copy-start | bytes 110596
  347.1 38.1 %all-to-all-start.1 = ((bf16[8,80,2304]{2,1,0:T(8,128)(2,1)}), bf16[8,80,2304]{2,1,0:T(8,128)(2,1)}, u32[]{:S(2)}, u32[]{:S(2)}) async-start(bf16[8,80,2304]{2,1,0:T(8,128)(2,1)} %bitcast.63), calls=%async_computation.1 | async-start | bytes 5898240 | tf_op jit(solution)/shard_map/all_to_all | solution.py:117
  352.8 107.1 %reduce-scatter.2.cloned.1.call-start = ((), (), s32[]{:S(2)}) async-start(), calls=%async_computation.3 | async-start | bytes 1327104 | tf_op jit(solution)/shard_map/reduce_scatter | solution.py:135
Sparse Core Ops, SparseCore 0:
  10.8 84.0 all-gather.6
  140.2 98.8 all-gather.4
  391.8 68.0 reduce-scatter.1
